TPU v7x, 32 devices: a whole 2x2x4 slice. The times are simulated.
32 devices in a mesh: tx: 8 (over z, y), ty: 4 (over x, core).
Axes of the slice: x: 2, y: 2, z: 4, core: 2. Of those that a mesh axis runs over, the one named last changes fastest.
Arguments:
- concentration: float32 [64, 64, 256], P('tx', 'ty'), may hold values from -6 to 6
- source: float32 [64, 64, 256], P('tx', 'ty'), may hold values from -4 to 4
- material: int32 [64, 64, 256], P('tx', 'ty'), may hold values from 0 to 7
Outputs:
- updated: float32 [64, 64, 256], P('tx', 'ty')
All inputs are finite; a program needn't handle non-finite values.
Results may differ from a plain program's by a relative error of at most 0.00017.
Values sent between devices are 32-bit elements; how exact they have to be, the bound alone decides.
No kernel may reach another device: no remote copies, remote signals or barrier semaphores. Data moves between devices by JAX's collectives and lax.ppermute only.
A program may use at most 128 MiB of HBM per device.

v0:
```python
import jax
import jax.numpy as jnp
from jax import lax
from jax.sharding import PartitionSpec as P

mass_rate = 0.001
relax_weight = 0.8
diffusivities = (0.15, 0.3, 0.5, 0.8, 1.2, 2.0, 3.2, 5.0)


def with_halo(cells, sides, width):
    for axis, dim in sides:
        count = lax.axis_size(axis)
        head = lax.slice_in_dim(cells, 0, width, axis=dim)
        tail = lax.slice_in_dim(cells, cells.shape[dim] - width, cells.shape[dim], axis=dim)
        cells = jnp.concatenate(
            [
                lax.ppermute(tail, axis, [(i, (i + 1) % count) for i in range(count)]),
                cells,
                lax.ppermute(head, axis, [((i + 1) % count, i) for i in range(count)]),
            ],
            axis=dim,
        )
    return cells


def lookup(material):
    result = jnp.zeros(material.shape, jnp.float32)
    for slot_id, coeff_value in enumerate(diffusivities):
        result = jnp.where(material == slot_id, jnp.float32(coeff_value), result)
    return result


def couplings(kappa_pad, scales):
    scale_x, scale_y, scale_z = scales
    centre = kappa_pad[1:-1, 1:-1]
    return [
        0.5 * scale_x * (centre + kappa_pad[2:, 1:-1]),
        0.5 * scale_x * (centre + kappa_pad[:-2, 1:-1]),
        0.5 * scale_y * (centre + kappa_pad[1:-1, 2:]),
        0.5 * scale_y * (centre + kappa_pad[1:-1, :-2]),
        0.5 * scale_z * (centre + jnp.roll(centre, -1, axis=2)),
        0.5 * scale_z * (centre + jnp.roll(centre, 1, axis=2)),
    ]


def diagonal_of(coupled):
    summed = mass_rate + coupled[0]
    for coupled_term in coupled[1:]:
        summed = summed + coupled_term
    return summed


def operate(field_pad, coupled, diagonal):
    centre = field_pad[1:-1, 1:-1]
    beside_all = (
        field_pad[2:, 1:-1],
        field_pad[:-2, 1:-1],
        field_pad[1:-1, 2:],
        field_pad[1:-1, :-2],
        jnp.roll(centre, -1, axis=2),
        jnp.roll(centre, 1, axis=2),
    )
    off_sum = coupled[0] * beside_all[0]
    for number in range(1, 6):
        off_sum = off_sum + coupled[number] * beside_all[number]
    return diagonal * centre - off_sum


def sweep(field_pad, forcing, coupled, diagonal):
    centre = field_pad[1:-1, 1:-1]
    return centre + relax_weight * (forcing - operate(field_pad, coupled, diagonal)) / diagonal


def restrict(cells, ratios=(2, 2, 2)):
    size_x, size_y, size_z = cells.shape
    ratio_x, ratio_y, ratio_z = ratios
    grouped = cells.reshape(
        size_x // ratio_x, ratio_x, size_y // ratio_y, ratio_y, size_z // ratio_z, ratio_z
    )
    return jnp.sum(grouped, axis=(1, 3, 5)) * (1.0 / (ratio_x * ratio_y * ratio_z))


def prolong(coarse, ratios=(2, 2, 2)):
    return jnp.repeat(jnp.repeat(jnp.repeat(coarse, ratios[0], 0), ratios[1], 1), ratios[2], 2)


def wrap_pad(cells):
    return jnp.pad(cells, ((1, 1), (1, 1), (0, 0)), mode="wrap")


def scales_of(spacing):
    return tuple((1.0 / (step_size * step_size) for step_size in spacing))


def next_ratios(shape):
    return tuple((2 for extent in shape))


def exact_solve(forcing, coupled, diagonal):
    shape = forcing.shape
    cells = forcing.size
    basis = jnp.eye(cells, dtype=forcing.dtype).reshape((cells,) + shape)
    matrix = jax.vmap(lambda unit: operate(wrap_pad(unit), coupled, diagonal).reshape(cells))(basis)
    factor = jnp.linalg.cholesky(matrix)
    solved = jax.scipy.linalg.cho_solve((factor, True), forcing.reshape(cells))
    return solved.reshape(shape)


def coarse_solve(forcing, kappa, spacing):
    coupled = couplings(wrap_pad(kappa), scales_of(spacing))
    diagonal = diagonal_of(coupled)
    ratios = next_ratios(forcing.shape)
    if forcing.size <= 64 or ratios == (1, 1, 1):
        return exact_solve(forcing, coupled, diagonal)
    current = relax_weight * forcing / diagonal
    current = sweep(wrap_pad(current), forcing, coupled, diagonal)
    residual = forcing - operate(wrap_pad(current), coupled, diagonal)
    wider = tuple((step_size * ratio for step_size, ratio in zip(spacing, ratios)))
    correction = coarse_solve(restrict(residual, ratios), restrict(kappa, ratios), wider)
    current = current + prolong(correction, ratios)
    for repeat in range(2):
        current = sweep(wrap_pad(current), forcing, coupled, diagonal)
    return current


def grid_rim(cells, rim_width):
    return with_halo(cells, (("tx", 0), ("ty", 1)), rim_width)


def grid_ops(kappa_two, scales):
    wide = couplings(kappa_two, scales)
    wide_diag = diagonal_of(wide)
    inner = [coupled_term[1:-1, 1:-1] for coupled_term in wide]
    return (wide, wide_diag, inner, wide_diag[1:-1, 1:-1])


def smooth_twice(current, forcing, operators):
    wide, wide_diag, inner, inner_diag = operators
    for repeat in range(2):
        current = sweep(grid_rim(current, 1), forcing, inner, inner_diag)
    return current


def descend(forcing, operators):
    inner, inner_diag = (operators[2], operators[3])
    current = relax_weight * forcing / inner_diag
    current = sweep(grid_rim(current, 1), forcing, inner, inner_diag)
    residual = forcing - operate(grid_rim(current, 1), inner, inner_diag)
    return (current, residual)


def fetch_coarse(forcing_tile, kappa_tile):
    along_y = (
        lax.all_gather(forcing_tile, "ty", axis=1, tiled=True),
        lax.all_gather(kappa_tile, "ty", axis=1, tiled=True),
    )
    whole = (
        lax.all_gather(along_y[0], "tx", axis=0, tiled=True),
        lax.all_gather(along_y[1], "tx", axis=0, tiled=True),
    )
    return (whole[0], whole[1])


def shards(concentration, source, material):
    kappa_wide = with_halo(lookup(material), (("tx", 0), ("ty", 1)), 8)
    kappa_mid = restrict(kappa_wide)
    kappa_low = restrict(kappa_mid)
    kappa_base = restrict(kappa_low)
    top_ops = grid_ops(kappa_wide[6:-6, 6:-6], (1.0, 1.0, 1.0))
    mid_ops = grid_ops(kappa_mid[2:-2, 2:-2], (0.25, 0.25, 0.25))
    low_ops = grid_ops(kappa_low, (0.0625, 0.0625, 0.0625))
    forcing_top = mass_rate * concentration + source
    current_top = smooth_twice(concentration, forcing_top, top_ops)
    residual_top = forcing_top - operate(grid_rim(current_top, 1), top_ops[2], top_ops[3])
    forcing_mid = restrict(residual_top)
    current_mid, residual_mid = descend(forcing_mid, mid_ops)
    forcing_low = restrict(residual_mid)
    current_low, residual_low = descend(forcing_low, low_ops)
    forcing_base = restrict(residual_low)
    forcing_whole, kappa_whole = fetch_coarse(forcing_base, kappa_base[1:-1, 1:-1])
    solved_whole = coarse_solve(forcing_whole, kappa_whole, (8.0, 8.0, 8.0))
    part_x, part_y, part_z = forcing_base.shape
    start_x = lax.axis_index("tx") * part_x
    start_y = lax.axis_index("ty") * part_y
    current_base = lax.dynamic_slice(
        solved_whole, (start_x, start_y, jnp.int32(0)), (part_x, part_y, part_z)
    )
    current_low = current_low + prolong(current_base)
    current_low = smooth_twice(current_low, forcing_low, low_ops)
    current_mid = current_mid + prolong(current_low)
    current_mid = smooth_twice(current_mid, forcing_mid, mid_ops)
    current_top = current_top + prolong(current_mid)
    return smooth_twice(current_top, forcing_top, top_ops)


def solution(mesh):
    placed = (P("tx", "ty", None), P("tx", "ty", None), P("tx", "ty", None))
    return jax.shard_map(
        shards, mesh=mesh, in_specs=placed, out_specs=P("tx", "ty", None), check_vma=False
    )
```

profile of v0, /device:TPU:0, one launch (start us, length us, event | category | flops | bytes accessed | tf_op | source)
XLA Modules:
  0.0 330.1 jit_solution(3862219390328763433)
XLA Ops:
  1.0 3.0 collective-permute-start
  4.1 3.1 collective-permute-start.1
  7.9 4.7 %collective-permute-start.4 = (f32[1,16,256]{2,1,0:T(8,128)S(1)}, f32[1,16,256]{2,1,0:T(8,128)S(1)}, u32[]{:S(2)}, u32[]{:S(2)}) collective-permute-start(f32[1,16,256]{2,1,0:T(8,128)S(1)} %get-tuple-element.71), channel_id=1, source_target_pairs={{4,0},{8,4},{12,8},{16,12},{20,16},{24,20},{28,24},{0,28},{5,1},{9... | collective-permute-start | bytes 49160 | tf_op jit(solution)/shard_map/ppermute | solution.py:20
  20.1 3.0 collective-permute-done.2
  25.8 51.6 %reshape.179 = f32[12,2,16,2,128,2]{5,4,3,2,1,0:T(8,128)} reshape(f32[24,32,256]{2,1,0:T(8,128)S(1)} %pad_maximum_fusion) | data formatting | bytes 1572864 | tf_op jit(solution)/shard_map/reshape | solution.py:78
  77.4 17.8 %reduce_sum.98 = f32[12,16,128]{2,1,0:T(8,128)S(1)} reduce(f32[12,2,16,2,128,2]{5,4,3,2,1,0:T(8,128)} %reshape.179, f32[]{:T(128)} %constant.121.clone.1), dimensions={1,3,5}, to_apply=%region_1.2 | reduce | flops 172032 | bytes 884740 | tf_op jit(solution)/shard_map/reduce_sum | solution.py:81
  96.1 7.6 %mul.837 = f32[6,2,8,2,64,2]{5,4,3,2,1,0:T(8,128)} reshape(f32[12,16,128]{2,1,0:T(8,128)S(1)} %broadcast_multiply_fusion) | data formatting | bytes 196608 | tf_op jit(solution)/shard_map/mul | solution.py:81
  103.7 3.3 reduce_sum.100
  109.3 5.3 %all_gather.14 = f32[1,8,32]{2,0,1:T(1,128)S(1)} all-gather(f32[1,2,32]{2,0,1:T(1,128)S(1)} %bitcast.82), channel_id=1, replica_groups=mesh['tx'=8,'ty'=4] {'ty'}, dimensions={1}, use_global_device_ids=true | all-gather | bytes 1280 | tf_op jit(solution)/shard_map/all_gather | solution.py:156
  114.7 30.6 %all_gather.15 = f32[8,8,32]{2,1,0:T(8,128)S(1)} all-gather(f32[1,8,32]{2,1,0:T(8,128)S(1)} %bitcast.76), channel_id=1, replica_groups=mesh['tx'=8,'ty'=4] {'tx'}, dimensions={0}, use_global_device_ids=true | all-gather | bytes 9216 | tf_op jit(solution)/shard_map/all_gather | solution.py:160
  151.2 2.9 cholesky.16
  157.7 3.1 custom-call.10
  161.0 4.2 %collective-permute-start.12 = (f32[1,16,256]{2,1,0:T(8,128)S(1)}, f32[1,16,256]{2,1,0:T(8,128)S(1)}, u32[]{:S(2)}, u32[]{:S(2)}) collective-permute-start(f32[1,16,256]{2,1,0:T(8,128)S(1)} %get-tuple-element.60), channel_id=1, source_target_pairs={{4,0},{8,4},{12,8},{16,12},{20,16},{24,20},{28,24},{0,28},{5,1},{9... | collective-permute-start | bytes 49160 | tf_op jit(solution)/shard_map/ppermute | solution.py:20
  166.7 5.0 %collective-permute-done.13 = f32[1,16,256]{2,1,0:T(8,128)S(1)} collective-permute-done((f32[1,16,256]{2,1,0:T(8,128)S(1)}, f32[1,16,256]{2,1,0:T(8,128)S(1)}, u32[]{:S(2)}, u32[]{:S(2)}) %collective-permute-start.13) | collective-permute-done | bytes 16416 | tf_op jit(solution)/shard_map/ppermute | solution.py:18
  175.2 9.8 %reshape.178 = f32[4,2,8,2,128,2]{5,4,3,2,1,0:T(8,128)} reshape(f32[8,16,256]{2,1,0:T(8,128)S(1)} %fusion.41) | data formatting | bytes 262144 | tf_op jit(solution)/shard_map/reshape | solution.py:78
  185.0 4.0 %reduce_sum.97 = f32[4,8,128]{2,1,0:T(8,128)S(1)} reduce(f32[4,2,8,2,128,2]{5,4,3,2,1,0:T(8,128)} %reshape.178, f32[]{:T(128)} %constant.121.clone.1), dimensions={1,3,5}, to_apply=%region_0.1 | reduce | flops 28672 | bytes 147460 | tf_op jit(solution)/shard_map/reduce_sum | solution.py:81
  192.8 2.8 collective-permute-done.17
  202.4 2.8 collective-permute-done.21
  213.2 2.9 collective-permute-done.25
  223.0 2.8 collective-permute-done.29
  229.2 5.1 %all-gather.2 = f32[4,2,32]{2,1,0:T(2,128)S(1)} all-gather(f32[1,2,32]{2,1,0:T(2,128)S(1)} %multiply_bitcast_fusion), channel_id=2, replica_groups=mesh['tx'=8,'ty'=4] {'ty'}, dimensions={0}, use_global_device_ids=true | all-gather | bytes 1280 | tf_op jit(solution)/shard_map/all_gather | solution.py:155
  234.2 30.6 %all-gather.1 = f32[64,32]{1,0:T(8,128)S(1)} all-gather(f32[8,32]{1,0:T(8,128)S(1)} %bitcast.77), channel_id=3, replica_groups=mesh['tx'=8,'ty'=4] {'tx'}, dimensions={0}, use_global_device_ids=true | all-gather | bytes 9216 | tf_op jit(solution)/shard_map/all_gather | solution.py:159
  269.9 2.0 collective-permute-start.33
  273.4 2.8 collective-permute-done.33
  283.1 2.8 collective-permute-done.37
  289.4 2.0 collective-permute-start.41
  293.0 2.8 collective-permute-done.41
  299.0 2.0 collective-permute-start.45
  302.6 2.8 collective-permute-done.45
  313.1 2.8 collective-permute-done.49
  319.5 2.0 collective-permute-start.53
  323.2 2.8 collective-permute-done.53
  (333 shorter events, 98.4 us)
Async XLA Ops:
  1.0 16.6 %collective-permute-start = (f32[8,16,256]{2,1,0:T(8,128)S(1)}, f32[8,16,256]{2,1,0:T(8,128)S(1)}, u32[]{:S(2)}, u32[]{:S(2)}) collective-permute-start(f32[8,16,256]{2,1,0:T(8,128)S(1)} %select_select_fusion), channel_id=1, source_target_pairs={{0,4},{4,8},{8,12},{12,16},{16,20},{20,24},{24,28},{28,0},{1,5},{5... | collective-permute-start | bytes 393224 | tf_op jit(solution)/shard_map/ppermute | solution.py:18
  4.1 13.5 %collective-permute-start.1 = (f32[8,16,256]{2,1,0:T(8,128)S(1)}, f32[8,16,256]{2,1,0:T(8,128)S(1)}, u32[]{:S(2)}, u32[]{:S(2)}) collective-permute-start(f32[8,16,256]{2,1,0:T(8,128)S(1)} %select_select_fusion), channel_id=1, source_target_pairs={{4,0},{8,4},{12,8},{16,12},{20,16},{24,20},{28,24},{0,28},{5,1},{9... | collective-permute-start | bytes 393224 | tf_op jit(solution)/shard_map/ppermute | solution.py:20
  7.9 8.7 %collective-permute-start.5 = (f32[1,16,256]{2,1,0:T(8,128)S(1)}, f32[1,16,256]{2,1,0:T(8,128)S(1)}, u32[]{:S(2)}, u32[]{:S(2)}) collective-permute-start(f32[1,16,256]{2,1,0:T(8,128)S(1)} %get-tuple-element.72), channel_id=1, source_target_pairs={{0,4},{4,8},{8,12},{12,16},{16,20},{20,24},{24,28},{28,0},{1,5},{5... | collective-permute-start | bytes 49160 | tf_op jit(solution)/shard_map/ppermute | solution.py:18
  7.9 9.6 %collective-permute-start.4 = (f32[1,16,256]{2,1,0:T(8,128)S(1)}, f32[1,16,256]{2,1,0:T(8,128)S(1)}, u32[]{:S(2)}, u32[]{:S(2)}) collective-permute-start(f32[1,16,256]{2,1,0:T(8,128)S(1)} %get-tuple-element.71), channel_id=1, source_target_pairs={{4,0},{8,4},{12,8},{16,12},{20,16},{24,20},{28,24},{0,28},{5,1},{9... | collective-permute-start | bytes 49160 | tf_op jit(solution)/shard_map/ppermute | solution.py:20
  17.7 5.4 %collective-permute-start.2 = (f32[24,8,256]{2,1,0:T(8,128)S(1)}, f32[24,8,256]{2,1,0:T(8,128)S(1)}, u32[]{:S(2)}, u32[]{:S(2)}) collective-permute-start(f32[24,8,256]{2,1,0:T(8,128)S(1)} %get-tuple-element.31), channel_id=1, source_target_pairs={{0,1},{1,2},{2,3},{3,0},{4,5},{5,6},{6,7},{7,4},{8,9},{9,10},{10,1... | collective-permute-start | bytes 589832 | tf_op jit(solution)/shard_map/ppermute | solution.py:18
  17.8 6.4 %collective-permute-start.3 = (f32[24,8,256]{2,1,0:T(8,128)S(1)}, f32[24,8,256]{2,1,0:T(8,128)S(1)}, u32[]{:S(2)}, u32[]{:S(2)}) collective-permute-start(f32[24,8,256]{2,1,0:T(8,128)S(1)} %get-tuple-element.32), channel_id=1, source_target_pairs={{1,0},{2,1},{3,2},{0,3},{5,4},{6,5},{7,6},{4,7},{9,8},{10,9},{11,1... | collective-permute-start | bytes 589832 | tf_op jit(solution)/shard_map/ppermute | solution.py:20
  19.5 5.2 %collective-permute-start.6 = (f32[10,1,256]{2,1,0:T(1,128)S(1)}, f32[10,1,256]{2,1,0:T(1,128)S(1)}, u32[]{:S(2)}, u32[]{:S(2)}) collective-permute-start(f32[10,1,256]{2,1,0:T(1,128)S(1)} %get-tuple-element.41), channel_id=1, source_target_pairs={{1,0},{2,1},{3,2},{0,3},{5,4},{6,5},{7,6},{4,7},{9,8},{10,9},{11,1... | collective-permute-start | bytes 30728 | tf_op jit(solution)/shard_map/ppermute | solution.py:20
  19.6 5.2 %collective-permute-start.7 = (f32[10,1,256]{2,1,0:T(1,128)S(1)}, f32[10,1,256]{2,1,0:T(1,128)S(1)}, u32[]{:S(2)}, u32[]{:S(2)}) collective-permute-start(f32[10,1,256]{2,1,0:T(1,128)S(1)} %get-tuple-element.42), channel_id=1, source_target_pairs={{0,1},{1,2},{2,3},{3,0},{4,5},{5,6},{6,7},{7,4},{8,9},{9,10},{10,1... | collective-permute-start | bytes 30728 | tf_op jit(solution)/shard_map/ppermute | solution.py:18
  148.8 8.3 %collective-permute-start.8 = (f32[1,16,256]{2,1,0:T(8,128)}, f32[1,16,256]{2,1,0:T(8,128)S(1)}, u32[]{:S(2)}, u32[]{:S(2)}) collective-permute-start(f32[1,16,256]{2,1,0:T(8,128)} %get-tuple-element.66), channel_id=1, source_target_pairs={{4,0},{8,4},{12,8},{16,12},{20,16},{24,20},{28,24},{0,28},{5,1},{9... | collective-permute-start | bytes 49160 | tf_op jit(solution)/shard_map/ppermute | solution.py:20
  150.3 6.8 %collective-permute-start.9 = (f32[1,16,256]{2,1,0:T(8,128)}, f32[1,16,256]{2,1,0:T(8,128)S(1)}, u32[]{:S(2)}, u32[]{:S(2)}) collective-permute-start(f32[1,16,256]{2,1,0:T(8,128)} %get-tuple-element.65), channel_id=1, source_target_pairs={{0,4},{4,8},{8,12},{12,16},{16,20},{20,24},{24,28},{28,0},{1,5},{5... | collective-permute-start | bytes 49160 | tf_op jit(solution)/shard_map/ppermute | solution.py:18
  157.1 3.6 %collective-permute-start.10 = (f32[10,1,256]{2,1,0:T(1,128)S(1)}, f32[10,1,256]{2,1,0:T(1,128)S(1)}, u32[]{:S(2)}, u32[]{:S(2)}) collective-permute-start(f32[10,1,256]{2,1,0:T(1,128)S(1)} %get-tuple-element.39), channel_id=1, source_target_pairs={{1,0},{2,1},{3,2},{0,3},{5,4},{6,5},{7,6},{4,7},{9,8},{10,9},{11,1... | collective-permute-start | bytes 30728 | tf_op jit(solution)/shard_map/ppermute | solution.py:20
  161.0 5.7 %collective-permute-start.12 = (f32[1,16,256]{2,1,0:T(8,128)S(1)}, f32[1,16,256]{2,1,0:T(8,128)S(1)}, u32[]{:S(2)}, u32[]{:S(2)}) collective-permute-start(f32[1,16,256]{2,1,0:T(8,128)S(1)} %get-tuple-element.60), channel_id=1, source_target_pairs={{4,0},{8,4},{12,8},{16,12},{20,16},{24,20},{28,24},{0,28},{5,1},{9... | collective-permute-start | bytes 49160 | tf_op jit(solution)/shard_map/ppermute | solution.py:20
  165.3 6.4 %collective-permute-start.13 = (f32[1,16,256]{2,1,0:T(8,128)S(1)}, f32[1,16,256]{2,1,0:T(8,128)S(1)}, u32[]{:S(2)}, u32[]{:S(2)}) collective-permute-start(f32[1,16,256]{2,1,0:T(8,128)S(1)} %get-tuple-element.59), channel_id=1, source_target_pairs={{0,4},{4,8},{8,12},{12,16},{16,20},{20,24},{24,28},{28,0},{1,5},{5... | collective-permute-start | bytes 49160 | tf_op jit(solution)/shard_map/ppermute | solution.py:18
  189.1 3.7 %collective-permute-start.16 = (f32[1,8,128]{2,1,0:T(8,128)S(1)}, f32[1,8,128]{2,1,0:T(8,128)S(1)}, u32[]{:S(2)}, u32[]{:S(2)}) collective-permute-start(f32[1,8,128]{2,1,0:T(8,128)S(1)} %get-tuple-element.162), channel_id=1, source_target_pairs={{4,0},{8,4},{12,8},{16,12},{20,16},{24,20},{28,24},{0,28},{5,1},{9... | collective-permute-start | bytes 12296 | tf_op jit(solution)/shard_map/ppermute | solution.py:20
  189.2 6.3 %collective-permute-start.17 = (f32[1,8,128]{2,1,0:T(8,128)S(1)}, f32[1,8,128]{2,1,0:T(8,128)S(1)}, u32[]{:S(2)}, u32[]{:S(2)}) collective-permute-start(f32[1,8,128]{2,1,0:T(8,128)S(1)} %get-tuple-element.161), channel_id=1, source_target_pairs={{0,4},{4,8},{8,12},{12,16},{16,20},{20,24},{24,28},{28,0},{1,5},{5... | collective-permute-start | bytes 12296 | tf_op jit(solution)/shard_map/ppermute | solution.py:18
  198.7 3.7 %collective-permute-start.20 = (f32[1,8,128]{2,1,0:T(8,128)S(1)}, f32[1,8,128]{2,1,0:T(8,128)S(1)}, u32[]{:S(2)}, u32[]{:S(2)}) collective-permute-start(f32[1,8,128]{2,1,0:T(8,128)S(1)} %get-tuple-element.156), channel_id=1, source_target_pairs={{4,0},{8,4},{12,8},{16,12},{20,16},{24,20},{28,24},{0,28},{5,1},{9... | collective-permute-start | bytes 12296 | tf_op jit(solution)/shard_map/ppermute | solution.py:20
  198.8 6.3 %collective-permute-start.21 = (f32[1,8,128]{2,1,0:T(8,128)S(1)}, f32[1,8,128]{2,1,0:T(8,128)S(1)}, u32[]{:S(2)}, u32[]{:S(2)}) collective-permute-start(f32[1,8,128]{2,1,0:T(8,128)S(1)} %get-tuple-element.155), channel_id=1, source_target_pairs={{0,4},{4,8},{8,12},{12,16},{16,20},{20,24},{24,28},{28,0},{1,5},{5... | collective-permute-start | bytes 12296 | tf_op jit(solution)/shard_map/ppermute | solution.py:18
  209.5 3.6 %collective-permute-start.24 = (f32[1,4,64]{2,1,0:T(4,128)S(1)}, f32[1,4,64]{2,1,0:T(4,128)S(1)}, u32[]{:S(2)}, u32[]{:S(2)}) collective-permute-start(f32[1,4,64]{2,1,0:T(4,128)S(1)} %get-tuple-element.226), channel_id=1, source_target_pairs={{4,0},{8,4},{12,8},{16,12},{20,16},{24,20},{28,24},{0,28},{5,1},{9... | collective-permute-start | bytes 3080 | tf_op jit(solution)/shard_map/ppermute | solution.py:20
  209.8 6.3 %collective-permute-start.25 = (f32[1,4,64]{2,1,0:T(4,128)S(1)}, f32[1,4,64]{2,1,0:T(4,128)S(1)}, u32[]{:S(2)}, u32[]{:S(2)}) collective-permute-start(f32[1,4,64]{2,1,0:T(4,128)S(1)} %get-tuple-element.225), channel_id=1, source_target_pairs={{0,4},{4,8},{8,12},{12,16},{16,20},{20,24},{24,28},{28,0},{1,5},{5... | collective-permute-start | bytes 3080 | tf_op jit(solution)/shard_map/ppermute | solution.py:18
  219.3 3.6 %collective-permute-start.28 = (f32[1,4,64]{2,1,0:T(4,128)S(1)}, f32[1,4,64]{2,1,0:T(4,128)S(1)}, u32[]{:S(2)}, u32[]{:S(2)}) collective-permute-start(f32[1,4,64]{2,1,0:T(4,128)S(1)} %get-tuple-element.216), channel_id=1, source_target_pairs={{4,0},{8,4},{12,8},{16,12},{20,16},{24,20},{28,24},{0,28},{5,1},{9... | collective-permute-start | bytes 3080 | tf_op jit(solution)/shard_map/ppermute | solution.py:20
  219.4 6.3 %collective-permute-start.29 = (f32[1,4,64]{2,1,0:T(4,128)S(1)}, f32[1,4,64]{2,1,0:T(4,128)S(1)}, u32[]{:S(2)}, u32[]{:S(2)}) collective-permute-start(f32[1,4,64]{2,1,0:T(4,128)S(1)} %get-tuple-element.215), channel_id=1, source_target_pairs={{0,4},{4,8},{8,12},{12,16},{16,20},{20,24},{24,28},{28,0},{1,5},{5... | collective-permute-start | bytes 3080 | tf_op jit(solution)/shard_map/ppermute | solution.py:18
  269.8 3.6 %collective-permute-start.32 = (f32[1,4,64]{2,1,0:T(4,128)S(1)}, f32[1,4,64]{2,1,0:T(4,128)S(1)}, u32[]{:S(2)}, u32[]{:S(2)}) collective-permute-start(f32[1,4,64]{2,1,0:T(4,128)S(1)} %get-tuple-element.212), channel_id=1, source_target_pairs={{4,0},{8,4},{12,8},{16,12},{20,16},{24,20},{28,24},{0,28},{5,1},{9... | collective-permute-start | bytes 3080 | tf_op jit(solution)/shard_map/ppermute | solution.py:20
  269.9 6.3 %collective-permute-start.33 = (f32[1,4,64]{2,1,0:T(4,128)S(1)}, f32[1,4,64]{2,1,0:T(4,128)S(1)}, u32[]{:S(2)}, u32[]{:S(2)}) collective-permute-start(f32[1,4,64]{2,1,0:T(4,128)S(1)} %get-tuple-element.211), channel_id=1, source_target_pairs={{0,4},{4,8},{8,12},{12,16},{16,20},{20,24},{24,28},{28,0},{1,5},{5... | collective-permute-start | bytes 3080 | tf_op jit(solution)/shard_map/ppermute | solution.py:18
  279.5 6.3 %collective-permute-start.37 = (f32[1,4,64]{2,1,0:T(4,128)S(1)}, f32[1,4,64]{2,1,0:T(4,128)S(1)}, u32[]{:S(2)}, u32[]{:S(2)}) collective-permute-start(f32[1,4,64]{2,1,0:T(4,128)S(1)} %get-tuple-element.205), channel_id=1, source_target_pairs={{0,4},{4,8},{8,12},{12,16},{16,20},{20,24},{24,28},{28,0},{1,5},{5... | collective-permute-start | bytes 3080 | tf_op jit(solution)/shard_map/ppermute | solution.py:18
  289.4 3.7 %collective-permute-start.40 = (f32[1,8,128]{2,1,0:T(8,128)S(1)}, f32[1,8,128]{2,1,0:T(8,128)S(1)}, u32[]{:S(2)}, u32[]{:S(2)}) collective-permute-start(f32[1,8,128]{2,1,0:T(8,128)S(1)} %get-tuple-element.144), channel_id=1, source_target_pairs={{4,0},{8,4},{12,8},{16,12},{20,16},{24,20},{28,24},{0,28},{5,1},{9... | collective-permute-start | bytes 12296 | tf_op jit(solution)/shard_map/ppermute | solution.py:20
  289.4 6.4 %collective-permute-start.41 = (f32[1,8,128]{2,1,0:T(8,128)S(1)}, f32[1,8,128]{2,1,0:T(8,128)S(1)}, u32[]{:S(2)}, u32[]{:S(2)}) collective-permute-start(f32[1,8,128]{2,1,0:T(8,128)S(1)} %get-tuple-element.143), channel_id=1, source_target_pairs={{0,4},{4,8},{8,12},{12,16},{16,20},{20,24},{24,28},{28,0},{1,5},{5... | collective-permute-start | bytes 12296 | tf_op jit(solution)/shard_map/ppermute | solution.py:18
  299.0 3.7 %collective-permute-start.44 = (f32[1,8,128]{2,1,0:T(8,128)S(1)}, f32[1,8,128]{2,1,0:T(8,128)S(1)}, u32[]{:S(2)}, u32[]{:S(2)}) collective-permute-start(f32[1,8,128]{2,1,0:T(8,128)S(1)} %get-tuple-element.138), channel_id=1, source_target_pairs={{4,0},{8,4},{12,8},{16,12},{20,16},{24,20},{28,24},{0,28},{5,1},{9... | collective-permute-start | bytes 12296 | tf_op jit(solution)/shard_map/ppermute | solution.py:20
  299.0 6.4 %collective-permute-start.45 = (f32[1,8,128]{2,1,0:T(8,128)S(1)}, f32[1,8,128]{2,1,0:T(8,128)S(1)}, u32[]{:S(2)}, u32[]{:S(2)}) collective-permute-start(f32[1,8,128]{2,1,0:T(8,128)S(1)} %get-tuple-element.137), channel_id=1, source_target_pairs={{0,4},{4,8},{8,12},{12,16},{16,20},{20,24},{24,28},{28,0},{1,5},{5... | collective-permute-start | bytes 12296 | tf_op jit(solution)/shard_map/ppermute | solution.py:18
  309.4 3.8 %collective-permute-start.48 = (f32[1,16,256]{2,1,0:T(8,128)S(1)}, f32[1,16,256]{2,1,0:T(8,128)S(1)}, u32[]{:S(2)}, u32[]{:S(2)}) collective-permute-start(f32[1,16,256]{2,1,0:T(8,128)S(1)} %get-tuple-element.54), channel_id=1, source_target_pairs={{4,0},{8,4},{12,8},{16,12},{20,16},{24,20},{28,24},{0,28},{5,1},{9... | collective-permute-start | bytes 49160 | tf_op jit(solution)/shard_map/ppermute | solution.py:20
  309.4 6.5 %collective-permute-start.49 = (f32[1,16,256]{2,1,0:T(8,128)S(1)}, f32[1,16,256]{2,1,0:T(8,128)S(1)}, u32[]{:S(2)}, u32[]{:S(2)}) collective-permute-start(f32[1,16,256]{2,1,0:T(8,128)S(1)} %get-tuple-element.53), channel_id=1, source_target_pairs={{0,4},{4,8},{8,12},{12,16},{16,20},{20,24},{24,28},{28,0},{1,5},{5... | collective-permute-start | bytes 49160 | tf_op jit(solution)/shard_map/ppermute | solution.py:18
  319.4 3.8 %collective-permute-start.52 = (f32[1,16,256]{2,1,0:T(8,128)S(1)}, f32[1,16,256]{2,1,0:T(8,128)S(1)}, u32[]{:S(2)}, u32[]{:S(2)}) collective-permute-start(f32[1,16,256]{2,1,0:T(8,128)S(1)} %get-tuple-element.48), channel_id=1, source_target_pairs={{4,0},{8,4},{12,8},{16,12},{20,16},{24,20},{28,24},{0,28},{5,1},{9... | collective-permute-start | bytes 49160 | tf_op jit(solution)/shard_map/ppermute | solution.py:20
  319.5 6.5 %collective-permute-start.53 = (f32[1,16,256]{2,1,0:T(8,128)S(1)}, f32[1,16,256]{2,1,0:T(8,128)S(1)}, u32[]{:S(2)}, u32[]{:S(2)}) collective-permute-start(f32[1,16,256]{2,1,0:T(8,128)S(1)} %get-tuple-element.47), channel_id=1, source_target_pairs={{0,4},{4,8},{8,12},{12,16},{16,20},{20,24},{24,28},{28,0},{1,5},{5... | collective-permute-start | bytes 49160 | tf_op jit(solution)/shard_map/ppermute | solution.py:18
  (44 other events, 1135.4 us)
where the time goes:
time: 331 us; the launch traced here: 330 us
  local copies, waits for them, and re-layouts  88 us (27%)
  waiting for transfers between devices  81.2 us (25%)
  blocking collectives  71.6 us (22%)
  starting transfers between devices  46.7 us (14%)
  other arithmetic  41.1 us (12%)
    reshape x6, local copies, waits for them, and re-layouts, restrict(): cells.reshape(size_x // ratio_x, ratio_x, size_y // ratio_y, ratio_y, siz...  63 us
    ppermute x28, waiting for transfers between devices, with_halo(): lax.ppermute(tail, axis, [(i, (i + 1) % count) for i in range(count)])  55.2 us
    all_gather x1, blocking collectives, fetch_coarse(): lax.all_gather(along_y[1], 'tx', axis=0, tiled=True)  30.6 us
    all_gather x1, blocking collectives, fetch_coarse(): lax.all_gather(along_y[0], 'tx', axis=0, tiled=True)  30.6 us
    ppermute x28, starting transfers between devices, with_halo(): lax.ppermute(tail, axis, [(i, (i + 1) % count) for i in range(count)])  29.9 us
    reduce_sum x11, other arithmetic, restrict(): jnp.sum(grouped, axis=(1, 3, 5)) * (1.0 / (ratio_x * ratio_y * ratio_z))  26 us
    ppermute x28, waiting for transfers between devices, with_halo(): lax.ppermute(head, axis, [((i + 1) % count, i) for i in range(count)])  25.9 us
    ppermute x28, starting transfers between devices, with_halo(): lax.ppermute(head, axis, [((i + 1) % count, i) for i in range(count)])  16.8 us
  transfers between devices with their start and end apart: 56, of which 46 were waited for; matrix products, arithmetic and copies ran while one was open for 5% of the time, Pallas kernels for 0%

commit v1 on v0

--- a/solution.py
+++ b/solution.py
@@ -6,6 +6,35 @@
 mass_rate = 0.001
 relax_weight = 0.8
 diffusivities = (0.15, 0.3, 0.5, 0.8, 1.2, 2.0, 3.2, 5.0)
+
+
+def recast_the_bars(mat, shard_axis):
+    step_out = lax.psum(1, shard_axis)
+    local_now = lax.axis_index(shard_axis)
+    item_now, z1, shaped = (step_out, local_now, mat.shape[0])
+    fresh = range(item_now)
+    finding = map(lambda k0: (k0, (k0 + 1) % item_now), fresh)
+    row_list = list(finding)
+    opened = range(item_now)
+    arr_next = map(lambda k0: (k0, (k0 - 1) % item_now), opened)
+    steps_seen = list(arr_next)
+    front = jnp.zeros((*mat.shape[:0], item_now * shaped, *mat.shape[1:]), mat.dtype)
+    front = lax.dynamic_update_slice_in_dim(front, mat, z1 * shaped, axis=0)
+    part_now = built = mat
+    then = item_now // 2
+    c = 1
+    while c < then + 1:
+        part_now = lax.ppermute(part_now, shard_axis, perm=row_list)
+        front = lax.dynamic_update_slice_in_dim(
+            front, part_now, (z1 - c) % item_now * shaped, axis=0
+        )
+        if c < item_now - then:
+            built = lax.ppermute(built, shard_axis, perm=steps_seen)
+            front = lax.dynamic_update_slice_in_dim(
+                front, built, (z1 + c) % item_now * shaped, axis=0
+            )
+        c = c + 1
+    return front
 
 
 def with_halo(cells, sides, width):
@@ -156,7 +185,7 @@
         lax.all_gather(kappa_tile, "ty", axis=1, tiled=True),
     )
     whole = (
-        lax.all_gather(along_y[0], "tx", axis=0, tiled=True),
+        recast_the_bars(along_y[0], shard_axis="tx"),
         lax.all_gather(along_y[1], "tx", axis=0, tiled=True),
     )
     return (whole[0], whole[1])

time: 331 us -> 343 us (1.036)
  blocking collectives: 71.6 us -> 41 us
  starting transfers between devices: 46.7 us -> 63.9 us
  other arithmetic: 41.1 us -> 50.4 us
  local copies, waits for them, and re-layouts: 88 us -> 97.2 us
  waiting for transfers between devices: 81.2 us -> 87.8 us
    all_gather x1 -> x0, blocking collectives: 30.6 us -> none  [fetch_coarse(): lax.all_gather(along_y[0], 'tx', axis=0, tiled=True)]
    ppermute x0 -> x7, starting transfers between devices: none -> 14.4 us  [the longest x3 14.4 us: recast_the_bars(): built = lax.ppermute(built, shard_axis, perm=steps_seen)]
    ppermute x28, starting transfers between devices: 16.8 us -> 21.8 us  [with_halo(): lax.ppermute(head, axis, [((i + 1) % count, i) for i in range(count)])]
    add x15 -> x16, other arithmetic: 2.63 us -> 7.16 us  [sweep(): centre + relax_weight * (forcing - operate(field_pad, coupled, diagonal))...]
    slice x14 -> x21, local copies, waits for them, and re-layouts: 0.65 us -> 4.89 us  [wrap_pad(): return jnp.pad(cells, ((1, 1), (1, 1), (0, 0)), mode='wrap')]
    ppermute x28, waiting for transfers between devices: 55.2 us -> 59.2 us  [with_halo(): lax.ppermute(tail, axis, [(i, (i + 1) % count) for i in range(count)])]
  transfers between devices with their start and end apart: 56 -> 63, of which waited for: 46 -> 52; matrix products, arithmetic and copies ran while one was open for 5% -> 8% of each run, Pallas kernels for 0% -> 0%
where the time goes in v1:
time: 343 us; the launch traced here: 342 us
  local copies, waits for them, and re-layouts  97.2 us (28%)
  waiting for transfers between devices  87.8 us (26%)
  starting transfers between devices  63.9 us (19%)
  other arithmetic  50.4 us (15%)
  blocking collectives  41 us (12%)
    reshape x6, local copies, waits for them, and re-layouts, restrict(): cells.reshape(size_x // ratio_x, ratio_x, size_y // ratio_y, ratio_y, siz...  63 us
    ppermute x28, waiting for transfers between devices, with_halo(): lax.ppermute(tail, axis, [(i, (i + 1) % count) for i in range(count)])  59.2 us
    all_gather x1, blocking collectives, fetch_coarse(): lax.all_gather(along_y[1], 'tx', axis=0, tiled=True)  30.6 us
    ppermute x28, starting transfers between devices, with_halo(): lax.ppermute(tail, axis, [(i, (i + 1) % count) for i in range(count)])  27.7 us
    reduce_sum x11, other arithmetic, restrict(): jnp.sum(grouped, axis=(1, 3, 5)) * (1.0 / (ratio_x * ratio_y * ratio_z))  26.7 us
    ppermute x28, waiting for transfers between devices, with_halo(): lax.ppermute(head, axis, [((i + 1) % count, i) for i in range(count)])  25.9 us
    ppermute x28, starting transfers between devices, with_halo(): lax.ppermute(head, axis, [((i + 1) % count, i) for i in range(count)])  21.8 us
    ppermute x3, starting transfers between devices, recast_the_bars(): built = lax.ppermute(built, shard_axis, perm=steps_seen)  14.4 us
  transfers between devices with their start and end apart: 63, of which 52 were waited for; matrix products, arithmetic and copies ran while one was open for 8% of the time, Pallas kernels for 0%

profile of v1, /device:TPU:0, one launch (start us, length us, event | category | flops | bytes accessed | tf_op | source)
XLA Modules:
  0.0 342.1 jit_solution(822182566495040133)
XLA Ops:
  1.0 3.0 collective-permute-start
  4.1 3.1 collective-permute-start.1
  7.9 4.7 %collective-permute-start.4 = (f32[1,16,256]{2,1,0:T(8,128)S(1)}, f32[1,16,256]{2,1,0:T(8,128)S(1)}, u32[]{:S(2)}, u32[]{:S(2)}) collective-permute-start(f32[1,16,256]{2,1,0:T(8,128)S(1)} %get-tuple-element.107), channel_id=1, source_target_pairs={{4,0},{8,4},{12,8},{16,12},{20,16},{24,20},{28,24},{0,28},{5,1},{9... | collective-permute-start | bytes 49160 | tf_op jit(solution)/shard_map/ppermute | solution.py:49
  19.4 3.0 collective-permute-done.2
  25.2 51.6 %reshape.179 = f32[12,2,16,2,128,2]{5,4,3,2,1,0:T(8,128)} reshape(f32[24,32,256]{2,1,0:T(8,128)S(1)} %pad_maximum_fusion) | data formatting | bytes 1572864 | tf_op jit(solution)/shard_map/reshape | solution.py:107
  76.8 17.8 %reduce_sum.98 = f32[12,16,128]{2,1,0:T(8,128)S(1)} reduce(f32[12,2,16,2,128,2]{5,4,3,2,1,0:T(8,128)} %reshape.179, f32[]{:T(128)} %constant.162.clone.1), dimensions={1,3,5}, to_apply=%region_1.2 | reduce | flops 172032 | bytes 884740 | tf_op jit(solution)/shard_map/reduce_sum | solution.py:110
  95.4 7.7 %mul.837 = f32[6,2,8,2,64,2]{5,4,3,2,1,0:T(8,128)} reshape(f32[12,16,128]{2,1,0:T(8,128)S(1)} %broadcast_multiply_fusion) | data formatting | bytes 196608 | tf_op jit(solution)/shard_map/mul | solution.py:110
  103.0 3.3 reduce_sum.100
  108.6 5.3 %all_gather.10 = f32[1,8,32]{2,0,1:T(1,128)S(1)} all-gather(f32[1,2,32]{2,0,1:T(1,128)S(1)} %bitcast.82), channel_id=1, replica_groups=mesh['tx'=8,'ty'=4] {'ty'}, dimensions={1}, use_global_device_ids=true | all-gather | bytes 1280 | tf_op jit(solution)/shard_map/all_gather | solution.py:185
  114.0 30.6 %all_gather.11 = f32[8,8,32]{2,1,0:T(8,128)S(1)} all-gather(f32[1,8,32]{2,1,0:T(8,128)S(1)} %bitcast.76), channel_id=1, replica_groups=mesh['tx'=8,'ty'=4] {'tx'}, dimensions={0}, use_global_device_ids=true | all-gather | bytes 9216 | tf_op jit(solution)/shard_map/all_gather | solution.py:189
  147.2 2.1 collective-permute-start.8
  150.3 2.9 cholesky.16
  161.7 4.8 %collective-permute-start.12 = (f32[1,16,256]{2,1,0:T(8,128)S(1)}, f32[1,16,256]{2,1,0:T(8,128)S(1)}, u32[]{:S(2)}, u32[]{:S(2)}) collective-permute-start(f32[1,16,256]{2,1,0:T(8,128)S(1)} %get-tuple-element.96), channel_id=1, source_target_pairs={{4,0},{8,4},{12,8},{16,12},{20,16},{24,20},{28,24},{0,28},{5,1},{9... | collective-permute-start | bytes 49160 | tf_op jit(solution)/shard_map/ppermute | solution.py:49
  168.0 5.0 %collective-permute-done.13 = f32[1,16,256]{2,1,0:T(8,128)S(1)} collective-permute-done((f32[1,16,256]{2,1,0:T(8,128)S(1)}, f32[1,16,256]{2,1,0:T(8,128)S(1)}, u32[]{:S(2)}, u32[]{:S(2)}) %collective-permute-start.13) | collective-permute-done | bytes 16416 | tf_op jit(solution)/shard_map/ppermute | solution.py:47
  176.5 9.8 %reshape.178 = f32[4,2,8,2,128,2]{5,4,3,2,1,0:T(8,128)} reshape(f32[8,16,256]{2,1,0:T(8,128)S(1)} %fusion.92) | data formatting | bytes 262144 | tf_op jit(solution)/shard_map/reshape | solution.py:107
  186.3 4.0 %reduce_sum.97 = f32[4,8,128]{2,1,0:T(8,128)S(1)} reduce(f32[4,2,8,2,128,2]{5,4,3,2,1,0:T(8,128)} %reshape.178, f32[]{:T(128)} %constant.162.clone.1), dimensions={1,3,5}, to_apply=%region_0.1 | reduce | flops 28672 | bytes 147460 | tf_op jit(solution)/shard_map/reduce_sum | solution.py:110
  194.0 2.8 collective-permute-done.17
  203.6 2.8 collective-permute-done.21
  214.7 2.8 collective-permute-done.25
  225.0 2.8 collective-permute-done.29
  231.9 5.1 %all-gather.1 = f32[4,2,32]{2,1,0:T(2,128)S(1)} all-gather(f32[1,2,32]{2,1,0:T(2,128)S(1)} %multiply_bitcast_fusion), channel_id=2, replica_groups=mesh['tx'=8,'ty'=4] {'ty'}, dimensions={0}, use_global_device_ids=true | all-gather | bytes 1280 | tf_op jit(solution)/shard_map/all_gather | solution.py:184
  237.6 4.7 %collective-permute-start.33 = (f32[1,8,32]{2,1,0:T(8,128)S(1)}, f32[1,8,32]{2,1,0:T(8,128)S(1)}, u32[]{:S(2)}, u32[]{:S(2)}) collective-permute-start(f32[1,8,32]{2,1,0:T(8,128)S(1)} %bitcast.74), channel_id=1, source_target_pairs={{0,28},{4,0},{8,4},{12,8},{16,12},{20,16},{24,20},{28,24},{1,29},{... | collective-permute-start | bytes 3080 | tf_op jit(solution)/shard_map/ppermute | solution.py:32
  243.6 5.0 %collective-permute-start.35 = (f32[1,8,32]{2,1,0:T(8,128)S(1)}, f32[1,8,32]{2,1,0:T(8,128)S(1)}, u32[]{:S(2)}, u32[]{:S(2)}) collective-permute-start(f32[1,8,32]{2,1,0:T(8,128)S(1)} %collective-permute-done.33), channel_id=1, source_target_pairs={{0,28},{4,0},{8,4},{12,8},{16,12},{20,16},{24,20},{28,24},{1,29},{... | collective-permute-start | bytes 3080 | tf_op jit(solution)/shard_map/ppermute | solution.py:32
  254.0 4.7 %collective-permute-start.37 = (f32[1,8,32]{2,1,0:T(8,128)S(1)}, f32[1,8,32]{2,1,0:T(8,128)S(1)}, u32[]{:S(2)}, u32[]{:S(2)}) collective-permute-start(f32[1,8,32]{2,1,0:T(8,128)S(1)} %collective-permute-done.35), channel_id=1, source_target_pairs={{0,28},{4,0},{8,4},{12,8},{16,12},{20,16},{24,20},{28,24},{1,29},{... | collective-permute-start | bytes 3080 | tf_op jit(solution)/shard_map/ppermute | solution.py:32
  260.2 3.2 custom-call.10
  274.4 4.3 %collective-permute-start.39 = (f32[1,4,64]{2,1,0:T(4,128)S(1)}, f32[1,4,64]{2,1,0:T(4,128)S(1)}, u32[]{:S(2)}, u32[]{:S(2)}) collective-permute-start(f32[1,4,64]{2,1,0:T(4,128)S(1)} %get-tuple-element.228), channel_id=1, source_target_pairs={{4,0},{8,4},{12,8},{16,12},{20,16},{24,20},{28,24},{0,28},{5,1},{9... | collective-permute-start | bytes 3080 | tf_op jit(solution)/shard_map/ppermute | solution.py:49
  280.0 5.0 %collective-permute-done.40 = f32[1,4,64]{2,1,0:T(4,128)S(1)} collective-permute-done((f32[1,4,64]{2,1,0:T(4,128)S(1)}, f32[1,4,64]{2,1,0:T(4,128)S(1)}, u32[]{:S(2)}, u32[]{:S(2)}) %collective-permute-start.40) | collective-permute-done | bytes 1056 | tf_op jit(solution)/shard_map/ppermute | solution.py:47
  292.6 2.8 collective-permute-done.44
  303.4 2.8 collective-permute-done.48
  313.8 2.8 collective-permute-done.52
  325.2 2.8 collective-permute-done.56
  335.2 2.8 collective-permute-done.60
  (403 shorter events, 125.2 us)
Async XLA Ops:
  1.0 15.9 %collective-permute-start = (f32[8,16,256]{2,1,0:T(8,128)S(1)}, f32[8,16,256]{2,1,0:T(8,128)S(1)}, u32[]{:S(2)}, u32[]{:S(2)}) collective-permute-start(f32[8,16,256]{2,1,0:T(8,128)S(1)} %select_select_fusion), channel_id=1, source_target_pairs={{0,4},{4,8},{8,12},{12,16},{16,20},{20,24},{24,28},{28,0},{1,5},{5... | collective-permute-start | bytes 393224 | tf_op jit(solution)/shard_map/ppermute | solution.py:47
  4.1 12.9 %collective-permute-start.1 = (f32[8,16,256]{2,1,0:T(8,128)S(1)}, f32[8,16,256]{2,1,0:T(8,128)S(1)}, u32[]{:S(2)}, u32[]{:S(2)}) collective-permute-start(f32[8,16,256]{2,1,0:T(8,128)S(1)} %select_select_fusion), channel_id=1, source_target_pairs={{4,0},{8,4},{12,8},{16,12},{20,16},{24,20},{28,24},{0,28},{5,1},{9... | collective-permute-start | bytes 393224 | tf_op jit(solution)/shard_map/ppermute | solution.py:49
  7.9 8.1 %collective-permute-start.5 = (f32[1,16,256]{2,1,0:T(8,128)S(1)}, f32[1,16,256]{2,1,0:T(8,128)S(1)}, u32[]{:S(2)}, u32[]{:S(2)}) collective-permute-start(f32[1,16,256]{2,1,0:T(8,128)S(1)} %get-tuple-element.108), channel_id=1, source_target_pairs={{0,4},{4,8},{8,12},{12,16},{16,20},{20,24},{24,28},{28,0},{1,5},{5... | collective-permute-start | bytes 49160 | tf_op jit(solution)/shard_map/ppermute | solution.py:47
  7.9 9.0 %collective-permute-start.4 = (f32[1,16,256]{2,1,0:T(8,128)S(1)}, f32[1,16,256]{2,1,0:T(8,128)S(1)}, u32[]{:S(2)}, u32[]{:S(2)}) collective-permute-start(f32[1,16,256]{2,1,0:T(8,128)S(1)} %get-tuple-element.107), channel_id=1, source_target_pairs={{4,0},{8,4},{12,8},{16,12},{20,16},{24,20},{28,24},{0,28},{5,1},{9... | collective-permute-start | bytes 49160 | tf_op jit(solution)/shard_map/ppermute | solution.py:49
  17.0 5.4 %collective-permute-start.2 = (f32[24,8,256]{2,1,0:T(8,128)S(1)}, f32[24,8,256]{2,1,0:T(8,128)S(1)}, u32[]{:S(2)}, u32[]{:S(2)}) collective-permute-start(f32[24,8,256]{2,1,0:T(8,128)S(1)} %get-tuple-element.35), channel_id=1, source_target_pairs={{0,1},{1,2},{2,3},{3,0},{4,5},{5,6},{6,7},{7,4},{8,9},{9,10},{10,1... | collective-permute-start | bytes 589832 | tf_op jit(solution)/shard_map/ppermute | solution.py:47
  17.1 6.4 %collective-permute-start.3 = (f32[24,8,256]{2,1,0:T(8,128)S(1)}, f32[24,8,256]{2,1,0:T(8,128)S(1)}, u32[]{:S(2)}, u32[]{:S(2)}) collective-permute-start(f32[24,8,256]{2,1,0:T(8,128)S(1)} %get-tuple-element.36), channel_id=1, source_target_pairs={{1,0},{2,1},{3,2},{0,3},{5,4},{6,5},{7,6},{4,7},{9,8},{10,9},{11,1... | collective-permute-start | bytes 589832 | tf_op jit(solution)/shard_map/ppermute | solution.py:49
  18.9 5.2 %collective-permute-start.6 = (f32[10,1,256]{2,1,0:T(1,128)S(1)}, f32[10,1,256]{2,1,0:T(1,128)S(1)}, u32[]{:S(2)}, u32[]{:S(2)}) collective-permute-start(f32[10,1,256]{2,1,0:T(1,128)S(1)} %get-tuple-element.53), channel_id=1, source_target_pairs={{1,0},{2,1},{3,2},{0,3},{5,4},{6,5},{7,6},{4,7},{9,8},{10,9},{11,1... | collective-permute-start | bytes 30728 | tf_op jit(solution)/shard_map/ppermute | solution.py:49
  18.9 5.2 %collective-permute-start.7 = (f32[10,1,256]{2,1,0:T(1,128)S(1)}, f32[10,1,256]{2,1,0:T(1,128)S(1)}, u32[]{:S(2)}, u32[]{:S(2)}) collective-permute-start(f32[10,1,256]{2,1,0:T(1,128)S(1)} %get-tuple-element.54), channel_id=1, source_target_pairs={{0,1},{1,2},{2,3},{3,0},{4,5},{5,6},{6,7},{7,4},{8,9},{9,10},{10,1... | collective-permute-start | bytes 30728 | tf_op jit(solution)/shard_map/ppermute | solution.py:47
  147.2 11.1 %collective-permute-start.8 = (f32[1,16,256]{2,1,0:T(8,128)}, f32[1,16,256]{2,1,0:T(8,128)S(1)}, u32[]{:S(2)}, u32[]{:S(2)}) collective-permute-start(f32[1,16,256]{2,1,0:T(8,128)} %get-tuple-element.102), channel_id=1, source_target_pairs={{4,0},{8,4},{12,8},{16,12},{20,16},{24,20},{28,24},{0,28},{5,1},{9... | collective-permute-start | bytes 49160 | tf_op jit(solution)/shard_map/ppermute | solution.py:49
  149.3 8.9 %collective-permute-start.9 = (f32[1,16,256]{2,1,0:T(8,128)}, f32[1,16,256]{2,1,0:T(8,128)S(1)}, u32[]{:S(2)}, u32[]{:S(2)}) collective-permute-start(f32[1,16,256]{2,1,0:T(8,128)} %get-tuple-element.101), channel_id=1, source_target_pairs={{0,4},{4,8},{8,12},{12,16},{16,20},{20,24},{24,28},{28,0},{1,5},{5... | collective-permute-start | bytes 49160 | tf_op jit(solution)/shard_map/ppermute | solution.py:47
  161.7 6.2 %collective-permute-start.12 = (f32[1,16,256]{2,1,0:T(8,128)S(1)}, f32[1,16,256]{2,1,0:T(8,128)S(1)}, u32[]{:S(2)}, u32[]{:S(2)}) collective-permute-start(f32[1,16,256]{2,1,0:T(8,128)S(1)} %get-tuple-element.96), channel_id=1, source_target_pairs={{4,0},{8,4},{12,8},{16,12},{20,16},{24,20},{28,24},{0,28},{5,1},{9... | collective-permute-start | bytes 49160 | tf_op jit(solution)/shard_map/ppermute | solution.py:49
  166.5 6.4 %collective-permute-start.13 = (f32[1,16,256]{2,1,0:T(8,128)S(1)}, f32[1,16,256]{2,1,0:T(8,128)S(1)}, u32[]{:S(2)}, u32[]{:S(2)}) collective-permute-start(f32[1,16,256]{2,1,0:T(8,128)S(1)} %get-tuple-element.95), channel_id=1, source_target_pairs={{0,4},{4,8},{8,12},{12,16},{16,20},{20,24},{24,28},{28,0},{1,5},{5... | collective-permute-start | bytes 49160 | tf_op jit(solution)/shard_map/ppermute | solution.py:47
  190.4 6.4 %collective-permute-start.17 = (f32[1,8,128]{2,1,0:T(8,128)S(1)}, f32[1,8,128]{2,1,0:T(8,128)S(1)}, u32[]{:S(2)}, u32[]{:S(2)}) collective-permute-start(f32[1,8,128]{2,1,0:T(8,128)S(1)} %get-tuple-element.177), channel_id=1, source_target_pairs={{0,4},{4,8},{8,12},{12,16},{16,20},{20,24},{24,28},{28,0},{1,5},{5... | collective-permute-start | bytes 12296 | tf_op jit(solution)/shard_map/ppermute | solution.py:47
  200.0 6.4 %collective-permute-start.21 = (f32[1,8,128]{2,1,0:T(8,128)S(1)}, f32[1,8,128]{2,1,0:T(8,128)S(1)}, u32[]{:S(2)}, u32[]{:S(2)}) collective-permute-start(f32[1,8,128]{2,1,0:T(8,128)S(1)} %get-tuple-element.171), channel_id=1, source_target_pairs={{0,4},{4,8},{8,12},{12,16},{16,20},{20,24},{24,28},{28,0},{1,5},{5... | collective-permute-start | bytes 12296 | tf_op jit(solution)/shard_map/ppermute | solution.py:47
  211.1 6.3 %collective-permute-start.25 = (f32[1,4,64]{2,1,0:T(4,128)S(1)}, f32[1,4,64]{2,1,0:T(4,128)S(1)}, u32[]{:S(2)}, u32[]{:S(2)}) collective-permute-start(f32[1,4,64]{2,1,0:T(4,128)S(1)} %get-tuple-element.241), channel_id=1, source_target_pairs={{0,4},{4,8},{8,12},{12,16},{16,20},{20,24},{24,28},{28,0},{1,5},{5... | collective-permute-start | bytes 3080 | tf_op jit(solution)/shard_map/ppermute | solution.py:47
  221.4 6.3 %collective-permute-start.29 = (f32[1,4,64]{2,1,0:T(4,128)S(1)}, f32[1,4,64]{2,1,0:T(4,128)S(1)}, u32[]{:S(2)}, u32[]{:S(2)}) collective-permute-start(f32[1,4,64]{2,1,0:T(4,128)S(1)} %get-tuple-element.231), channel_id=1, source_target_pairs={{0,4},{4,8},{8,12},{12,16},{16,20},{20,24},{24,28},{28,0},{1,5},{5... | collective-permute-start | bytes 3080 | tf_op jit(solution)/shard_map/ppermute | solution.py:47
  237.0 6.3 %collective-permute-start.32 = (f32[1,8,32]{2,1,0:T(8,128)S(1)}, f32[1,8,32]{2,1,0:T(8,128)S(1)}, u32[]{:S(2)}, u32[]{:S(2)}) collective-permute-start(f32[1,8,32]{2,1,0:T(8,128)S(1)} %bitcast.73), channel_id=1, source_target_pairs={{0,4},{4,8},{8,12},{12,16},{16,20},{20,24},{24,28},{28,0},{1,5},{5... | collective-permute-start | bytes 3080 | tf_op jit(solution)/shard_map/ppermute | solution.py:27
  237.6 6.0 %collective-permute-start.33 = (f32[1,8,32]{2,1,0:T(8,128)S(1)}, f32[1,8,32]{2,1,0:T(8,128)S(1)}, u32[]{:S(2)}, u32[]{:S(2)}) collective-permute-start(f32[1,8,32]{2,1,0:T(8,128)S(1)} %bitcast.74), channel_id=1, source_target_pairs={{0,28},{4,0},{8,4},{12,8},{16,12},{20,16},{24,20},{28,24},{1,29},{... | collective-permute-start | bytes 3080 | tf_op jit(solution)/shard_map/ppermute | solution.py:32
  243.3 6.3 %collective-permute-start.34 = (f32[1,8,32]{2,1,0:T(8,128)S(1)}, f32[1,8,32]{2,1,0:T(8,128)S(1)}, u32[]{:S(2)}, u32[]{:S(2)}) collective-permute-start(f32[1,8,32]{2,1,0:T(8,128)S(1)} %collective-permute-done.32), channel_id=1, source_target_pairs={{0,4},{4,8},{8,12},{12,16},{16,20},{20,24},{24,28},{28,0},{1,5},{5... | collective-permute-start | bytes 3080 | tf_op jit(solution)/shard_map/ppermute | solution.py:27
  243.6 10.3 %collective-permute-start.35 = (f32[1,8,32]{2,1,0:T(8,128)S(1)}, f32[1,8,32]{2,1,0:T(8,128)S(1)}, u32[]{:S(2)}, u32[]{:S(2)}) collective-permute-start(f32[1,8,32]{2,1,0:T(8,128)S(1)} %collective-permute-done.33), channel_id=1, source_target_pairs={{0,28},{4,0},{8,4},{12,8},{16,12},{20,16},{24,20},{28,24},{1,29},{... | collective-permute-start | bytes 3080 | tf_op jit(solution)/shard_map/ppermute | solution.py:32
  249.6 9.1 %collective-permute-start.36 = (f32[1,8,32]{2,1,0:T(8,128)S(1)}, f32[1,8,32]{2,1,0:T(8,128)S(1)}, u32[]{:S(2)}, u32[]{:S(2)}) collective-permute-start(f32[1,8,32]{2,1,0:T(8,128)S(1)} %collective-permute-done.34), channel_id=1, source_target_pairs={{0,4},{4,8},{8,12},{12,16},{16,20},{20,24},{24,28},{28,0},{1,5},{5... | collective-permute-start | bytes 3080 | tf_op jit(solution)/shard_map/ppermute | solution.py:27
  254.0 10.4 %collective-permute-start.37 = (f32[1,8,32]{2,1,0:T(8,128)S(1)}, f32[1,8,32]{2,1,0:T(8,128)S(1)}, u32[]{:S(2)}, u32[]{:S(2)}) collective-permute-start(f32[1,8,32]{2,1,0:T(8,128)S(1)} %collective-permute-done.35), channel_id=1, source_target_pairs={{0,28},{4,0},{8,4},{12,8},{16,12},{20,16},{24,20},{28,24},{1,29},{... | collective-permute-start | bytes 3080 | tf_op jit(solution)/shard_map/ppermute | solution.py:32
  258.7 6.3 %collective-permute-start.38 = (f32[1,8,32]{2,1,0:T(8,128)S(1)}, f32[1,8,32]{2,1,0:T(8,128)S(1)}, u32[]{:S(2)}, u32[]{:S(2)}) collective-permute-start(f32[1,8,32]{2,1,0:T(8,128)S(1)} %collective-permute-done.36), channel_id=1, source_target_pairs={{0,4},{4,8},{8,12},{12,16},{16,20},{20,24},{24,28},{28,0},{1,5},{5... | collective-permute-start | bytes 3080 | tf_op jit(solution)/shard_map/ppermute | solution.py:27
  274.4 5.6 %collective-permute-start.39 = (f32[1,4,64]{2,1,0:T(4,128)S(1)}, f32[1,4,64]{2,1,0:T(4,128)S(1)}, u32[]{:S(2)}, u32[]{:S(2)}) collective-permute-start(f32[1,4,64]{2,1,0:T(4,128)S(1)} %get-tuple-element.228), channel_id=1, source_target_pairs={{4,0},{8,4},{12,8},{16,12},{20,16},{24,20},{28,24},{0,28},{5,1},{9... | collective-permute-start | bytes 3080 | tf_op jit(solution)/shard_map/ppermute | solution.py:49
  278.7 6.3 %collective-permute-start.40 = (f32[1,4,64]{2,1,0:T(4,128)S(1)}, f32[1,4,64]{2,1,0:T(4,128)S(1)}, u32[]{:S(2)}, u32[]{:S(2)}) collective-permute-start(f32[1,4,64]{2,1,0:T(4,128)S(1)} %get-tuple-element.227), channel_id=1, source_target_pairs={{0,4},{4,8},{8,12},{12,16},{16,20},{20,24},{24,28},{28,0},{1,5},{5... | collective-permute-start | bytes 3080 | tf_op jit(solution)/shard_map/ppermute | solution.py:47
  289.0 6.3 %collective-permute-start.44 = (f32[1,4,64]{2,1,0:T(4,128)S(1)}, f32[1,4,64]{2,1,0:T(4,128)S(1)}, u32[]{:S(2)}, u32[]{:S(2)}) collective-permute-start(f32[1,4,64]{2,1,0:T(4,128)S(1)} %get-tuple-element.221), channel_id=1, source_target_pairs={{0,4},{4,8},{8,12},{12,16},{16,20},{20,24},{24,28},{28,0},{1,5},{5... | collective-permute-start | bytes 3080 | tf_op jit(solution)/shard_map/ppermute | solution.py:47
  299.8 6.4 %collective-permute-start.48 = (f32[1,8,128]{2,1,0:T(8,128)S(1)}, f32[1,8,128]{2,1,0:T(8,128)S(1)}, u32[]{:S(2)}, u32[]{:S(2)}) collective-permute-start(f32[1,8,128]{2,1,0:T(8,128)S(1)} %get-tuple-element.159), channel_id=1, source_target_pairs={{0,4},{4,8},{8,12},{12,16},{16,20},{20,24},{24,28},{28,0},{1,5},{5... | collective-permute-start | bytes 12296 | tf_op jit(solution)/shard_map/ppermute | solution.py:47
  310.2 6.4 %collective-permute-start.52 = (f32[1,8,128]{2,1,0:T(8,128)S(1)}, f32[1,8,128]{2,1,0:T(8,128)S(1)}, u32[]{:S(2)}, u32[]{:S(2)}) collective-permute-start(f32[1,8,128]{2,1,0:T(8,128)S(1)} %get-tuple-element.153), channel_id=1, source_target_pairs={{0,4},{4,8},{8,12},{12,16},{16,20},{20,24},{24,28},{28,0},{1,5},{5... | collective-permute-start | bytes 12296 | tf_op jit(solution)/shard_map/ppermute | solution.py:47
  321.4 3.8 %collective-permute-start.55 = (f32[1,16,256]{2,1,0:T(8,128)S(1)}, f32[1,16,256]{2,1,0:T(8,128)S(1)}, u32[]{:S(2)}, u32[]{:S(2)}) collective-permute-start(f32[1,16,256]{2,1,0:T(8,128)S(1)} %get-tuple-element.66), channel_id=1, source_target_pairs={{4,0},{8,4},{12,8},{16,12},{20,16},{24,20},{28,24},{0,28},{5,1},{9... | collective-permute-start | bytes 49160 | tf_op jit(solution)/shard_map/ppermute | solution.py:49
  321.4 6.5 %collective-permute-start.56 = (f32[1,16,256]{2,1,0:T(8,128)S(1)}, f32[1,16,256]{2,1,0:T(8,128)S(1)}, u32[]{:S(2)}, u32[]{:S(2)}) collective-permute-start(f32[1,16,256]{2,1,0:T(8,128)S(1)} %get-tuple-element.65), channel_id=1, source_target_pairs={{0,4},{4,8},{8,12},{12,16},{16,20},{20,24},{24,28},{28,0},{1,5},{5... | collective-permute-start | bytes 49160 | tf_op jit(solution)/shard_map/ppermute | solution.py:47
  331.4 3.8 %collective-permute-start.59 = (f32[1,16,256]{2,1,0:T(8,128)S(1)}, f32[1,16,256]{2,1,0:T(8,128)S(1)}, u32[]{:S(2)}, u32[]{:S(2)}) collective-permute-start(f32[1,16,256]{2,1,0:T(8,128)S(1)} %get-tuple-element.60), channel_id=1, source_target_pairs={{4,0},{8,4},{12,8},{16,12},{20,16},{24,20},{28,24},{0,28},{5,1},{9... | collective-permute-start | bytes 49160 | tf_op jit(solution)/shard_map/ppermute | solution.py:49
  331.5 6.5 %collective-permute-start.60 = (f32[1,16,256]{2,1,0:T(8,128)S(1)}, f32[1,16,256]{2,1,0:T(8,128)S(1)}, u32[]{:S(2)}, u32[]{:S(2)}) collective-permute-start(f32[1,16,256]{2,1,0:T(8,128)S(1)} %get-tuple-element.59), channel_id=1, source_target_pairs={{0,4},{4,8},{8,12},{12,16},{16,20},{20,24},{24,28},{28,0},{1,5},{5... | collective-permute-start | bytes 49160 | tf_op jit(solution)/shard_map/ppermute | solution.py:47
  (61 other events, 1520.8 us)
